TPU v7x, 32 devices: a whole 2x2x4 slice. The times are simulated.
32 devices in a mesh: dp: 8 (over z, x), seq: 4 (over y, core).
Axes of the slice: x: 2, y: 2, z: 4, core: 2. Of those that a mesh axis runs over, the one named last changes fastest.
Arguments:
- tokens: float32 [16, 256, 1024], P('dp', 'seq'), may hold values from -6 to 6
- output_cotangent: float32 [16, 256, 1024], P('dp', 'seq'), may hold values from -0.5 to 0.5
- placement: int32 [8], replicated, may hold values from 0 to 15, as said below
- inward: float32 [1024, 3072], P(('dp', 'seq'))
- outward: float32 [1024, 1024], P(('dp', 'seq')), may hold values from -0.75 to 0.75
- attend_vectors: float32 [5, 1024], P(None, ('dp', 'seq'))
- expand: float32 [1024, 4096], P(('dp', 'seq')), may hold values from -0.1875 to 0.1875
- shrink: float32 [4096, 1024], P(('dp', 'seq')), may hold values from -0.09375 to 0.09375
- feed_vectors: float32 [3, 1024], P(None, ('dp', 'seq'))
- expand_bias: float32 [4096], P(('dp', 'seq')), may hold values from -3 to 3
- inward_moments: float32 [2, 1024, 3072], P(None, ('dp', 'seq')), as said below
- outward_moments: float32 [2, 1024, 1024], P(None, ('dp', 'seq'))
- attend_moments: float32 [2, 5, 1024], P(None, None, ('dp', 'seq'))
- expand_moments: float32 [2, 1024, 4096], P(None, ('dp', 'seq'))
- shrink_moments: float32 [2, 4096, 1024], P(None, ('dp', 'seq'))
- feed_moments: float32 [2, 3, 1024], P(None, None, ('dp', 'seq'))
- bias_moments: float32 [2, 4096], P(None, ('dp', 'seq'))
Outputs:
- block_output: float32 [16, 256, 1024], P('dp', 'seq')
- input_gradient: float32 [16, 256, 1024], P('dp', 'seq')
- inward_gradient: float32 [1024, 3072], P(('dp', 'seq'))
- outward_gradient: float32 [1024, 1024], P(('dp', 'seq'))
- attend_gradient: float32 [5, 1024], P(None, ('dp', 'seq'))
- expand_gradient: float32 [1024, 4096], P(('dp', 'seq'))
- shrink_gradient: float32 [4096, 1024], P(('dp', 'seq'))
- feed_gradient: float32 [3, 1024], P(None, ('dp', 'seq'))
- bias_gradient: float32 [4096], P(('dp', 'seq'))
- inward_new: float32 [1024, 3072], P(('dp', 'seq'))
- outward_new: float32 [1024, 1024], P(('dp', 'seq'))
- attend_new: float32 [5, 1024], P(None, ('dp', 'seq'))
- expand_new: float32 [1024, 4096], P(('dp', 'seq'))
- shrink_new: float32 [4096, 1024], P(('dp', 'seq'))
- feed_new: float32 [3, 1024], P(None, ('dp', 'seq'))
- bias_new: float32 [4096], P(('dp', 'seq'))
- inward_state: float32 [2, 1024, 3072], P(None, ('dp', 'seq'))
- outward_state: float32 [2, 1024, 1024], P(None, ('dp', 'seq'))
- attend_state: float32 [2, 5, 1024], P(None, None, ('dp', 'seq'))
- expand_state: float32 [2, 1024, 4096], P(None, ('dp', 'seq'))
- shrink_state: float32 [2, 4096, 1024], P(None, ('dp', 'seq'))
- feed_state: float32 [2, 3, 1024], P(None, None, ('dp', 'seq'))
- bias_state: float32 [2, 4096], P(None, ('dp', 'seq'))
Inputs may be any that keep to these rules, and one draw needn't show every extreme that they name: `placement`: entries are distinct slot numbers; slot s belongs to index s // 2 of dp; in every draw some index of dp holds 2 sequences. `inward_moments`: the second moment (index 1) is positive.
All inputs are finite; a program needn't handle non-finite values.
Results may differ from a plain program's by a relative error of at most 0.012.
Values may be sent and summed in bfloat16 or wider, within the bound.
A program may use at most 192 MiB of HBM per device.

v0:
```python
import math
import jax
import jax.numpy as jnp
from jax import lax
from jax.sharding import PartitionSpec as P

HEADS = 16
HEAD_DIM = 64
norm_epsilon = 1e-05
beta_first = 0.9
beta_second = 0.95
adam_epsilon = 1e-08
learn_rate = 0.01
weight_decay = 0.1
adam_steps = 4
gelu_scale = 0.7978845608028654
gelu_cubic = 0.044715
masked_score = -1e30


def halved(operand):
    return operand.astype(jnp.bfloat16)


def normalize(operand):
    average = jnp.mean(operand, axis=-1, keepdims=True)
    centered = operand - average
    variance = jnp.mean(centered * centered, axis=-1, keepdims=True)
    inverse = lax.rsqrt(variance + norm_epsilon)
    return (centered * inverse, inverse)


def norm_back(upstream, normed, inverse):
    first_mean = jnp.mean(upstream, axis=-1, keepdims=True)
    second_mean = jnp.mean(upstream * normed, axis=-1, keepdims=True)
    return inverse * (upstream - first_mean - normed * second_mean)


def gelu_pair(upper):
    inner_arg = gelu_scale * (upper + gelu_cubic * upper * upper * upper)
    tangent = jnp.tanh(inner_arg)
    active = 0.5 * upper * (1.0 + tangent)
    slope = 0.5 * (1.0 + tangent) + 0.5 * upper * (1.0 - tangent * tangent) * gelu_scale * (
        1.0 + 3.0 * gelu_cubic * upper * upper
    )
    return (active, slope)


def adamw_update(parameter, gradient, moments, decay_rate):
    first_moment = beta_first * moments[0] + (1.0 - beta_first) * gradient
    second = beta_second * moments[1] + (1.0 - beta_second) * gradient * gradient
    unbiased_first = first_moment / (1.0 - beta_first**adam_steps)
    unbiased_second = second / (1.0 - beta_second**adam_steps)
    update = unbiased_first / (jnp.sqrt(unbiased_second) + adam_epsilon) + decay_rate * parameter
    return (parameter - learn_rate * update, jnp.stack([first_moment, second]))


def lifted_fold(normed, pieces):
    weight_piece, vector_piece = pieces
    vector_float = vector_piece.astype(jnp.float32)
    lift_piece = halved(normed * vector_float[:, 0] + vector_float[:, 1])
    total = jnp.dot(lift_piece, weight_piece, preferred_element_type=jnp.float32)
    return (total, lift_piece, vector_float)


def body(
    tokens,
    output_cotangent,
    placement,
    inward,
    outward,
    attend_vectors,
    expand,
    shrink,
    feed_vectors,
    expand_bias,
    inward_moments,
    outward_moments,
    attend_moments,
    expand_moments,
    shrink_moments,
    feed_moments,
    bias_moments,
):
    slot_count, block_size, model_width = tokens.shape
    length = block_size * lax.axis_size("seq")
    row_count = slot_count * block_size
    score_scale = 1.0 / math.sqrt(HEAD_DIM)
    slot_ids = lax.axis_index("dp") * slot_count + jnp.arange(slot_count, dtype=jnp.int32)
    live_mask = jnp.any(placement[None, :] == slot_ids[:, None], axis=1).astype(jnp.float32)[
        :, None, None
    ]
    flat_tokens = tokens.reshape(row_count, model_width)
    normed_one, inverse_one = normalize(flat_tokens)
    attend_cols = halved(attend_vectors).T
    feed_cols = halved(feed_vectors).T
    packed, lifted_one, vec_rows_one = lifted_fold(
        normed_one,
        (
            lax.all_gather(halved(inward), ("dp", "seq"), axis=0, tiled=True),
            lax.all_gather(attend_cols, ("dp", "seq"), axis=0, tiled=True),
        ),
    )
    vec_one = vec_rows_one.T
    queries = halved(packed[:, :model_width] + vec_one[2]).reshape(
        slot_count, block_size, HEADS, HEAD_DIM
    )
    key_local = halved(packed[:, model_width : 2 * model_width]).reshape(
        slot_count, block_size, model_width
    )
    value_local = halved(packed[:, 2 * model_width :] + vec_one[3]).reshape(
        slot_count, block_size, model_width
    )
    key_whole, value_whole = (
        lax.all_gather(key_local, "seq", axis=1, tiled=True),
        lax.all_gather(value_local, "seq", axis=1, tiled=True),
    )
    key_heads = key_whole.reshape(slot_count, length, HEADS, HEAD_DIM)
    value_heads = value_whole.reshape(slot_count, length, HEADS, HEAD_DIM)
    query_pos = lax.axis_index("seq") * block_size + jnp.arange(block_size)
    allowed = jnp.arange(length)[None, :] <= query_pos[:, None]
    scores = (
        jnp.einsum("sqhd,skhd->shqk", queries, key_heads, preferred_element_type=jnp.float32)
        * score_scale
    )
    scores = jnp.where(allowed, scores, masked_score)
    score_peak = jnp.max(scores, axis=-1, keepdims=True)
    log_total = score_peak + jnp.log(jnp.sum(jnp.exp(scores - score_peak), axis=-1, keepdims=True))
    weights_half = halved(jnp.exp(scores - log_total))
    attended = halved(
        jnp.einsum(
            "shqk,skhd->sqhd", weights_half, value_heads, preferred_element_type=jnp.float32
        ).reshape(row_count, model_width)
    )
    projected = jnp.dot(
        attended,
        lax.all_gather(halved(outward), ("dp", "seq"), axis=0, tiled=True),
        preferred_element_type=jnp.float32,
    )
    middle = flat_tokens + projected + vec_one[4]
    normed_two, inverse_two = normalize(middle)
    upper_raw, lifted_two, vec_rows_two = lifted_fold(
        normed_two,
        (
            lax.all_gather(halved(expand), ("dp", "seq"), axis=0, tiled=True),
            lax.all_gather(feed_cols, ("dp", "seq"), axis=0, tiled=True),
        ),
    )
    vec_two = vec_rows_two.T
    weight_piece = lax.all_gather(halved(shrink), ("dp", "seq"), axis=0, tiled=True)
    bias_piece = lax.all_gather(halved(expand_bias), ("dp", "seq"), axis=0, tiled=True)
    bias_float = bias_piece.astype(jnp.float32)
    upper_cols = upper_raw + bias_float
    act_cols, unused_slope = gelu_pair(upper_cols)
    act_half = halved(act_cols)
    total = jnp.dot(act_half, weight_piece, preferred_element_type=jnp.float32)
    upper_act = upper_raw + bias_float
    unused_active, gelu_slope = gelu_pair(upper_act)
    result = middle + total + vec_two[2]
    block_output = result.reshape(slot_count, block_size, model_width) * live_mask
    cotangent = (output_cotangent * live_mask).reshape(row_count, model_width)
    cot_half = halved(cotangent)
    shrink_grad = jnp.dot(act_half.T, cot_half, preferred_element_type=jnp.float32)
    feed_bias_grad = jnp.sum(cotangent, axis=0)
    upper_grad = (
        jnp.dot(
            cot_half,
            lax.all_gather(halved(shrink), ("dp", "seq"), axis=0, tiled=True).T,
            preferred_element_type=jnp.float32,
        )
        * gelu_slope
    )
    upper_half = halved(upper_grad)
    expand_grad = jnp.dot(lifted_two.T, upper_half, preferred_element_type=jnp.float32)
    expand_bias_grad = jnp.sum(upper_grad, axis=0)
    lift_two_grad = jnp.dot(
        upper_half,
        lax.all_gather(halved(expand), ("dp", "seq"), axis=0, tiled=True).T,
        preferred_element_type=jnp.float32,
    )
    gain_two_grad = jnp.sum(lift_two_grad * normed_two, axis=0)
    shift_two_grad = jnp.sum(lift_two_grad, axis=0)
    middle_grad = cotangent + norm_back(lift_two_grad * vec_two[0], normed_two, inverse_two)
    feed_vec_grad = jnp.stack([gain_two_grad, shift_two_grad, feed_bias_grad], axis=1)
    feed_parts = (
        lax.psum_scatter(expand_grad, ("dp", "seq"), scatter_dimension=0, tiled=True),
        lax.psum_scatter(shrink_grad, ("dp", "seq"), scatter_dimension=0, tiled=True),
        lax.psum_scatter(feed_vec_grad, ("dp", "seq"), scatter_dimension=0, tiled=True),
        lax.psum_scatter(expand_bias_grad, ("dp", "seq"), scatter_dimension=0, tiled=True),
    )
    middle_half = halved(middle_grad)
    outward_grad = jnp.dot(attended.T, middle_half, preferred_element_type=jnp.float32)
    out_bias_grad = jnp.sum(middle_grad, axis=0)
    attended_back = jnp.dot(
        middle_half,
        lax.all_gather(halved(outward), ("dp", "seq"), axis=0, tiled=True).T,
        preferred_element_type=jnp.float32,
    )
    attended_grad = halved(attended_back).reshape(slot_count, block_size, HEADS, HEAD_DIM)
    attended_heads = attended.reshape(slot_count, block_size, HEADS, HEAD_DIM)
    delta_sum = jnp.sum(
        attended_grad.astype(jnp.float32) * attended_heads.astype(jnp.float32), axis=-1
    )
    scores_again = (
        jnp.einsum("sqhd,skhd->shqk", queries, key_heads, preferred_element_type=jnp.float32)
        * score_scale
    )
    scores_again = jnp.where(allowed, scores_again, masked_score)
    weights_full = jnp.exp(scores_again - log_total)
    weights_again = halved(weights_full)
    weight_grad = jnp.einsum(
        "sqhd,skhd->shqk", attended_grad, value_heads, preferred_element_type=jnp.float32
    )
    score_grad = halved(
        weights_full * (weight_grad - jnp.transpose(delta_sum, (0, 2, 1))[..., None]) * score_scale
    )
    query_grad = jnp.einsum(
        "shqk,skhd->sqhd", score_grad, key_heads, preferred_element_type=jnp.float32
    ).reshape(row_count, model_width)
    key_term = jnp.einsum(
        "shqk,sqhd->skhd", score_grad, queries, preferred_element_type=jnp.float32
    ).reshape(slot_count, length, model_width)
    value_term = jnp.einsum(
        "shqk,sqhd->skhd", weights_again, attended_grad, preferred_element_type=jnp.float32
    ).reshape(slot_count, length, model_width)
    key_grad, value_grad = (
        lax.psum_scatter(
            key_term.astype(jnp.bfloat16), "seq", scatter_dimension=1, tiled=True
        ).astype(jnp.float32),
        lax.psum_scatter(
            value_term.astype(jnp.bfloat16), "seq", scatter_dimension=1, tiled=True
        ).astype(jnp.float32),
    )
    key_grad = key_grad.reshape(row_count, model_width)
    value_grad = value_grad.reshape(row_count, model_width)
    packed_grad = halved(jnp.concatenate([query_grad, key_grad, value_grad], axis=1))
    inward_grad = jnp.dot(lifted_one.T, packed_grad, preferred_element_type=jnp.float32)
    query_bias_grad = jnp.sum(query_grad, axis=0)
    value_bias_grad = jnp.sum(value_grad, axis=0)
    lift_one_grad = jnp.dot(
        packed_grad,
        lax.all_gather(halved(inward), ("dp", "seq"), axis=0, tiled=True).T,
        preferred_element_type=jnp.float32,
    )
    gain_one_grad = jnp.sum(lift_one_grad * normed_one, axis=0)
    shift_one_grad = jnp.sum(lift_one_grad, axis=0)
    tokens_grad = middle_grad + norm_back(lift_one_grad * vec_one[0], normed_one, inverse_one)
    input_gradient = tokens_grad.reshape(slot_count, block_size, model_width) * live_mask
    attend_vec_grad = jnp.stack(
        [gain_one_grad, shift_one_grad, query_bias_grad, value_bias_grad, out_bias_grad], axis=1
    )
    attend_parts = (
        lax.psum_scatter(inward_grad, ("dp", "seq"), scatter_dimension=0, tiled=True),
        lax.psum_scatter(outward_grad, ("dp", "seq"), scatter_dimension=0, tiled=True),
        lax.psum_scatter(attend_vec_grad, ("dp", "seq"), scatter_dimension=0, tiled=True),
    )
    attend_vec_sum = attend_parts[2].T
    feed_vec_sum = feed_parts[2].T
    inward_new, inward_state = adamw_update(inward, attend_parts[0], inward_moments, weight_decay)
    outward_new, outward_state = adamw_update(
        outward, attend_parts[1], outward_moments, weight_decay
    )
    attend_new, attend_state = adamw_update(attend_vectors, attend_vec_sum, attend_moments, 0.0)
    expand_new, expand_state = adamw_update(expand, feed_parts[0], expand_moments, weight_decay)
    shrink_new, shrink_state = adamw_update(shrink, feed_parts[1], shrink_moments, weight_decay)
    feed_new, feed_state = adamw_update(feed_vectors, feed_vec_sum, feed_moments, 0.0)
    bias_new, bias_state = adamw_update(expand_bias, feed_parts[3], bias_moments, 0.0)
    return (
        block_output,
        input_gradient,
        attend_parts[0],
        attend_parts[1],
        attend_vec_sum,
        feed_parts[0],
        feed_parts[1],
        feed_vec_sum,
        feed_parts[3],
        inward_new,
        outward_new,
        attend_new,
        expand_new,
        shrink_new,
        feed_new,
        bias_new,
        inward_state,
        outward_state,
        attend_state,
        expand_state,
        shrink_state,
        feed_state,
        bias_state,
    )


def solution(mesh):
    placed = (
        P("dp", "seq", None),
        P("dp", "seq", None),
        P(),
        P(("dp", "seq"), None),
        P(("dp", "seq"), None),
        P(None, ("dp", "seq")),
        P(("dp", "seq"), None),
        P(("dp", "seq"), None),
        P(None, ("dp", "seq")),
        P(("dp", "seq")),
        P(None, ("dp", "seq"), None),
        P(None, ("dp", "seq"), None),
        P(None, None, ("dp", "seq")),
        P(None, ("dp", "seq"), None),
        P(None, ("dp", "seq"), None),
        P(None, None, ("dp", "seq")),
        P(None, ("dp", "seq")),
    )
    return jax.shard_map(
        body,
        mesh=mesh,
        in_specs=placed,
        out_specs=(
            P("dp", "seq", None),
            P("dp", "seq", None),
            P(("dp", "seq"), None),
            P(("dp", "seq"), None),
            P(None, ("dp", "seq")),
            P(("dp", "seq"), None),
            P(("dp", "seq"), None),
            P(None, ("dp", "seq")),
            P(("dp", "seq")),
            P(("dp", "seq"), None),
            P(("dp", "seq"), None),
            P(None, ("dp", "seq")),
            P(("dp", "seq"), None),
            P(("dp", "seq"), None),
            P(None, ("dp", "seq")),
            P(("dp", "seq")),
            P(None, ("dp", "seq"), None),
            P(None, ("dp", "seq"), None),
            P(None, None, ("dp", "seq")),
            P(None, ("dp", "seq"), None),
            P(None, ("dp", "seq"), None),
            P(None, None, ("dp", "seq")),
            P(None, ("dp", "seq")),
        ),
        check_vma=False,
    )
```

profile of v0, /device:TPU:9, one launch (start us, length us, event | category | flops | bytes accessed | tf_op | source)
XLA Modules:
  0.0 1384.8 jit_solution(13482467230646633061)
XLA Ops:
  9.8 36.3 %all-gather = bf16[32,32,5]{1,2,0:T(8,128)(2,1)S(1)} all-gather(bf16[1,32,5]{1,2,0:T(8,128)(2,1)S(1)} %convert_bitcast_fusion), channel_id=1, replica_groups=mesh['dp'=8,'seq'=4] {'dp','seq'}, dimensions={0}, use_global_device_ids=true | all-gather | bytes 10560 | tf_op jit(solution)/shard_map/all_gather | solution.py:101
  49.6 32.9 %all-gather.10.cloned.1.call-done = bf16[1024,3072]{1,0:T(8,128)(2,1)} async-done(((bf16[32,3072]{1,0:T(8,128)(2,1)}), bf16[1024,3072]{1,0:T(8,128)(2,1)}) %all-gather.10.cloned.1.call-update) | async-done | bytes 6291472 | tf_op jit(solution)/shard_map/all_gather | solution.py:100
  89.6 33.0 %all-gather.1 = bf16[32,32,3]{1,2,0:T(4,128)(2,1)S(1)} all-gather(bf16[1,32,3]{1,2,0:T(4,128)(2,1)S(1)} %convert_bitcast_fusion.1), channel_id=1, replica_groups=mesh['dp'=8,'seq'=4] {'dp','seq'}, dimensions={0}, use_global_device_ids=true | all-gather | bytes 6336 | tf_op jit(solution)/shard_map/all_gather | solution.py:146
  122.7 36.5 %all-gather.2 = bf16[32,1,128]{2,1,0:T(2,128)(2,1)S(1)} all-gather(bf16[1,1,128]{2,1,0:T(2,128)(2,1)S(1)} %convert_bitcast_fusion.2), channel_id=1, replica_groups=mesh['dp'=8,'seq'=4] {'dp','seq'}, dimensions={0}, use_global_device_ids=true | all-gather | bytes 8448 | tf_op jit(solution)/shard_map/all_gather | solution.py:151
  175.8 4.3 all-gather.16.cloned.1.call-done
  182.6 77.8 %all-gather.18.cloned.1.call-done = bf16[1024,4096]{1,0:T(8,128)(2,1)} async-done(((bf16[32,4096]{1,0:T(8,128)(2,1)}), bf16[1024,4096]{1,0:T(8,128)(2,1)}) %all-gather.18.cloned.1.call-update) | async-done | bytes 8388624 | tf_op jit(solution)/shard_map/all_gather | solution.py:145
  260.3 4.8 convolution_add_fusion
  266.5 8.1 fusion.49
  274.7 183.9 %reduce-scatter.23.cloned.1.call-done = f32[128,1024]{1,0:T(8,128)} async-done(((f32[4096,1024]{1,0:T(8,128)}), f32[128,1024]{1,0:T(8,128)}) %reduce-scatter.23.cloned.1.call-update) | async-done | bytes 524304 | tf_op jit(solution)/shard_map/reduce_scatter | solution.py:187
  463.5 75.1 %all-gather.20.cloned.1.call-done = bf16[4096,1024]{1,0:T(8,128)(2,1)} async-done(((bf16[128,1024]{1,0:T(8,128)(2,1)}), bf16[4096,1024]{1,0:T(8,128)(2,1)}) %all-gather.20.cloned.1.call-update) | async-done | bytes 8388624 | tf_op jit(solution)/shard_map/all_gather | solution.py:150
  538.6 8.3 fusion.60
  546.9 7.4 multiply_reduce_fusion.1
  578.7 11.0 reduce-scatter.15.cloned.1.call-done
  589.6 27.4 %reduce-scatter.13.cloned.1.call-done = bf16[2,64,1024]{2,1,0:T(8,128)(2,1)} async-done(((bf16[2,256,1024]{2,1,0:T(8,128)(2,1)}), bf16[2,64,1024]{2,1,0:T(8,128)(2,1)}) %reduce-scatter.13.cloned.1.call-update) | async-done | bytes 262160 | tf_op jit(solution)/shard_map/reduce_scatter | solution.py:227
  617.0 6.1 multiply_reduce_fusion.2
  628.0 6.3 fusion.19
  635.6 8.2 fusion.14
  646.8 39.5 %all-reduce = f32[4096]{0:T(1024)S(1)} all-reduce(f32[4096]{0:T(1024)S(1)} %copy-done.42), channel_id=10, replica_groups=mesh['dp'=8,'seq'=4] {'dp','seq'}, use_global_device_ids=true, to_apply=%region_29.30.clone | all-reduce | flops 4096 | bytes 32768
  687.5 5.7 fusion.8
  693.3 38.3 %reduce-scatter.27.cloned.1.call-done = f32[32,3]{1,0:T(8,128)} async-done(((f32[1024,3]{1,0:T(8,128)}), f32[32,3]{1,0:T(8,128)}) %reduce-scatter.27.cloned.1.call-update) | async-done | bytes 400
  736.3 129.6 %reduce-scatter.25.cloned.1.call-done = f32[32,5]{1,0:T(8,128)} async-done(((f32[1024,5]{1,0:T(8,128)}), f32[32,5]{1,0:T(8,128)}) %reduce-scatter.25.cloned.1.call-update) | async-done | bytes 656
  867.9 138.4 %reduce-scatter.19.cloned.1.call-done = f32[32,1024]{1,0:T(8,128)} async-done(((f32[1024,1024]{1,0:T(8,128)}), f32[32,1024]{1,0:T(8,128)}) %reduce-scatter.19.cloned.1.call-update) | async-done | bytes 131088 | tf_op jit(solution)/shard_map/reduce_scatter | solution.py:254
  1008.8 176.5 %reduce-scatter.17.cloned.1.call-done = f32[32,3072]{1,0:T(8,128)} async-done(((f32[1024,3072]{1,0:T(8,128)}), f32[32,3072]{1,0:T(8,128)}) %reduce-scatter.17.cloned.1.call-update) | async-done | bytes 393232 | tf_op jit(solution)/shard_map/reduce_scatter | solution.py:253
  1188.3 186.7 %reduce-scatter.21.cloned.1.call-done = f32[32,4096]{1,0:T(8,128)} async-done(((f32[1024,4096]{1,0:T(8,128)}), f32[32,4096]{1,0:T(8,128)}) %reduce-scatter.21.cloned.1.call-update) | async-done | bytes 524304 | tf_op jit(solution)/shard_map/reduce_scatter | solution.py:186
  (246 shorter events, 88.0 us)
Async XLA Ops:
  7.2 75.3 %all-gather.10.cloned.1.call-start = ((), (), s32[]{:S(2)}) async-start(), calls=%async_computation.8 | async-start | bytes 6488064 | tf_op jit(solution)/shard_map/all_gather | solution.py:100
  9.0 154.9 %all-gather.12.cloned.1.call-start = ((), (), s32[]{:S(2)}) async-start(), calls=%async_computation.9 | async-start | bytes 1310720 | tf_op jit(solution)/shard_map/all_gather | solution.py:116
  86.3 73.6 %copy-start.61 = (s32[8]{0:T(128)S(1)}, s32[8]{0:T(128)}, u32[]{:S(2)}) copy-start(s32[8]{0:T(128)} %param.19) | copy-start | bytes 100
  87.1 79.3 %all-gather.14.cloned.1.call-start = ((), (), s32[]{:S(2)}) async-start(), calls=%async_computation.10 | async-start | bytes 1310720 | tf_op jit(solution)/shard_map/all_gather | solution.py:115
  87.9 92.1 %all-gather.16.cloned.1.call-start = ((), (), s32[]{:S(2)}) async-start(), calls=%async_computation.11 | async-start | bytes 2162688 | tf_op jit(solution)/shard_map/all_gather | solution.py:137
  88.7 171.7 %all-gather.18.cloned.1.call-start = ((), (), s32[]{:S(2)}) async-start(), calls=%async_computation.12 | async-start | bytes 8650752 | tf_op jit(solution)/shard_map/all_gather | solution.py:145
  89.5 369.1 %reduce-scatter.23.cloned.1.call-start = ((), (), s32[]{:S(2)}) async-start(), calls=%async_computation.19 | async-start | bytes 17301504 | tf_op jit(solution)/shard_map/reduce_scatter | solution.py:187
  182.3 371.9 %copy-start.32 = (f32[128]{0:T(128)}, f32[128]{0:T(128)S(1)}, u32[]{:S(2)}) copy-start(f32[128]{0:T(128)S(1)} %broadcast_multiply_fusion.8) | copy-start | bytes 1540
  182.5 82.6 %copy-start.34 = (f32[128]{0:T(128)}, f32[128]{0:T(128)S(1)}, u32[]{:S(2)}) copy-start(f32[128]{0:T(128)S(1)} %add_rsqrt_fusion.1) | copy-start | bytes 1540
  274.6 263.9 %all-gather.20.cloned.1.call-start = ((), (), s32[]{:S(2)}) async-start(), calls=%async_computation.13 | async-start | bytes 8650752 | tf_op jit(solution)/shard_map/all_gather | solution.py:150
  461.8 127.8 %reduce-scatter.15.cloned.1.call-start = ((), (), s32[]{:S(2)}) async-start(), calls=%async_computation.15 | async-start | bytes 1310720 | tf_op jit(solution)/shard_map/reduce_scatter | solution.py:230
  566.7 50.3 %reduce-scatter.13.cloned.1.call-start = ((), (), s32[]{:S(2)}) async-start(), calls=%async_computation.14 | async-start | bytes 1310720 | tf_op jit(solution)/shard_map/reduce_scatter | solution.py:227
  575.3 156.3 %reduce-scatter.27.cloned.1.call-start = ((), (), s32[]{:S(2)}) async-start(), calls=%async_computation.21 | async-start | bytes 540672
  578.4 287.5 %reduce-scatter.25.cloned.1.call-start = ((), (), s32[]{:S(2)}) async-start(), calls=%async_computation.20 | async-start | bytes 540672
  624.3 382.1 %reduce-scatter.19.cloned.1.call-start = ((), (), s32[]{:S(2)}) async-start(), calls=%async_computation.17 | async-start | bytes 4325376 | tf_op jit(solution)/shard_map/reduce_scatter | solution.py:254
  627.1 558.1 %reduce-scatter.17.cloned.1.call-start = ((), (), s32[]{:S(2)}) async-start(), calls=%async_computation.16 | async-start | bytes 12976128 | tf_op jit(solution)/shard_map/reduce_scatter | solution.py:253
  634.4 740.6 %reduce-scatter.21.cloned.1.call-start = ((), (), s32[]{:S(2)}) async-start(), calls=%async_computation.18 | async-start | bytes 17301504 | tf_op jit(solution)/shard_map/reduce_scatter | solution.py:186
  733.6 133.1 %copy-start.41 = (f32[5,32]{1,0:T(8,128)S(1)}, f32[5,32]{1,0:T(8,128)}, u32[]{:S(2)}) copy-start(f32[5,32]{1,0:T(8,128)} %param.22) | copy-start | bytes 1924
  733.6 272.8 %copy-start.29 = (f32[2,32,1024]{2,1,0:T(8,128)S(1)}, f32[2,32,1024]{2,1,0:T(8,128)}, u32[]{:S(2)}) copy-start(f32[2,32,1024]{2,1,0:T(8,128)} %param.28) | copy-start | bytes 786436
  735.1 450.2 %copy-start.20 = (f32[32,3072]{1,0:T(8,128)S(1)}, f32[32,3072]{1,0:T(8,128)}, u32[]{:S(2)}) copy-start(f32[32,3072]{1,0:T(8,128)} %param.20) | copy-start | bytes 1179652
  735.1 450.2 %copy-start.24 = (f32[2,32,3072]{2,1,0:T(8,128)S(1)}, f32[2,32,3072]{2,1,0:T(8,128)}, u32[]{:S(2)}) copy-start(f32[2,32,3072]{2,1,0:T(8,128)} %param.27) | copy-start | bytes 2359300
  866.7 320.6 %copy-start.40 = (f32[32,5]{0,1:T(8,128)}, f32[32,5]{0,1:T(8,128)S(1)}, u32[]{:S(2)}) copy-start(f32[32,5]{0,1:T(8,128)S(1)} %copy.118) | copy-start | bytes 1924
  1008.8 366.2 %copy-start.19 = (f32[32,4096]{1,0:T(8,128)S(1)}, f32[32,4096]{1,0:T(8,128)}, u32[]{:S(2)}) copy-start(f32[32,4096]{1,0:T(8,128)} %param.23) | copy-start | bytes 1572868
  1008.8 366.2 %copy-start.22 = (f32[2,32,4096]{2,1,0:T(8,128)S(1)}, f32[2,32,4096]{2,1,0:T(8,128)}, u32[]{:S(2)}) copy-start(f32[2,32,4096]{2,1,0:T(8,128)} %param.30) | copy-start | bytes 3145732
  (52 other events, 880.6 us)
Sparse Core Ops, SparseCore 0:
  11.5 70.9 all-gather.9
  87.3 15.2 all-gather.11
  104.7 16.6 all-gather.13
  124.7 55.3 all-gather.15
  183.4 76.9 all-gather.17
  274.8 183.8 reduce-scatter.22
  462.1 76.4 all-gather.19
  566.8 22.7 reduce-scatter.14
  592.2 24.7 reduce-scatter.12
  619.1 112.4 reduce-scatter.26
  734.4 131.4 reduce-scatter.24
  868.6 137.7 reduce-scatter.18
  1013.0 172.2 reduce-scatter.16
  1188.0 186.9 reduce-scatter.20
where the time goes:
time: 1390 us; the launch traced here: 1380 us
  waiting for transfers between devices  1080 us (78%)
  blocking collectives  145 us (10%)
  matrix products  74.3 us (5%)
  local copies, waits for them, and re-layouts  34.1 us (2%)
  other arithmetic  33.4 us (2%)
  between operations  14.6 us (1%)
    reduce_scatter x1, waiting for transfers between devices, body(): lax.psum_scatter(expand_grad, ('dp', 'seq'), scatter_dimension=0, tiled=T...  187 us
    reduce_scatter x1, waiting for transfers between devices, body(): lax.psum_scatter(shrink_grad, ('dp', 'seq'), scatter_dimension=0, tiled=T...  184 us
    reduce_scatter x1, waiting for transfers between devices, body(): lax.psum_scatter(inward_grad, ('dp', 'seq'), scatter_dimension=0, tiled=T...  176 us
    unnamed x16, waiting for transfers between devices  168 us
    reduce_scatter x1, waiting for transfers between devices, body(): lax.psum_scatter(outward_grad, ('dp', 'seq'), scatter_dimension=0, tiled=...  138 us
    all_gather x1, waiting for transfers between devices, body(): lax.all_gather(halved(expand), ('dp', 'seq'), axis=0, tiled=True)  77.8 us
    all_gather x1, waiting for transfers between devices, body(): lax.all_gather(halved(shrink), ('dp', 'seq'), axis=0, tiled=True)  75.1 us
    unnamed x1, blocking collectives  39.5 us
  transfers between devices with their start and end apart: 14, of which 12 were waited for; matrix products, arithmetic and copies ran while one was open for 6% of the time, Pallas kernels for 0%

commit v1 on v0

--- a/solution.py
+++ b/solution.py
@@ -1,8 +1,10 @@
+import functools
 import math
 import jax
 import jax.numpy as jnp
 from jax import lax
 from jax.sharding import PartitionSpec as P
+from jax.lax import axis_index, axis_size, ppermute
 
 HEADS = 16
 HEAD_DIM = 64
@@ -16,6 +18,25 @@
 gelu_scale = 0.7978845608028654
 gelu_cubic = 0.044715
 masked_score = -1e30
+
+
+def pair_series(local_array, net_axis, dim_at):
+    w_next = axis_size(net_axis)
+    f_next = axis_index(net_axis)
+    arr_out, clean = (w_next, f_next)
+    y2, current_block = (local_array, 1)
+    while current_block < arr_out:
+        all_rows = ppermute(
+            y2, net_axis, list(map(lambda p: (p, p ^ current_block), range(arr_out)))
+        )
+        near = jnp.concatenate([y2, all_rows], axis=dim_at)
+        kept_arr = jnp.concatenate([all_rows, y2], axis=dim_at)
+        y2 = jnp.where(clean & current_block == 0, near, kept_arr)
+        current_block = 2 * current_block
+    return y2
+
+
+spread_classes = functools.partial(pair_series, net_axis=("dp", "seq"), dim_at=0)
 
 
 def halved(operand):
@@ -142,7 +163,7 @@
     upper_raw, lifted_two, vec_rows_two = lifted_fold(
         normed_two,
         (
-            lax.all_gather(halved(expand), ("dp", "seq"), axis=0, tiled=True),
+            spread_classes(halved(expand)),
             lax.all_gather(feed_cols, ("dp", "seq"), axis=0, tiled=True),
         ),
     )

time: 1390 us -> 1620 us (1.17)
  blocking collectives: 145 us -> 315 us
  waiting for transfers between devices: 1080 us -> 1120 us
    all_gather x1, blocking collectives: 33 us -> 209 us  [body(): lax.all_gather(feed_cols, ('dp', 'seq'), axis=0, tiled=True)]
    ppermute x0 -> x5, waiting for transfers between devices: none -> 54 us  [pair_series(): ppermute(y2, net_axis, list(map(lambda p: (p, p ^ current_block), range(a...]
  transfers between devices with their start and end apart: 14 -> 19, of which waited for: 12 -> 13; matrix products, arithmetic and copies ran while one was open for 6% -> 6% of each run, Pallas kernels for 0% -> 0%
where the time goes in v1:
time: 1620 us; the launch traced here: 1610 us
  waiting for transfers between devices  1120 us (69%)
  blocking collectives  315 us (19%)
  matrix products  78.5 us (5%)
  other arithmetic  38.2 us (2%)
  local copies, waits for them, and re-layouts  36.9 us (2%)
    all_gather x1, blocking collectives, body(): lax.all_gather(feed_cols, ('dp', 'seq'), axis=0, tiled=True)  209 us
    reduce_scatter x1, waiting for transfers between devices, body(): lax.psum_scatter(shrink_grad, ('dp', 'seq'), scatter_dimension=0, tiled=T...  188 us
    reduce_scatter x1, waiting for transfers between devices, body(): lax.psum_scatter(expand_grad, ('dp', 'seq'), scatter_dimension=0, tiled=T...  187 us
    reduce_scatter x1, waiting for transfers between devices, body(): lax.psum_scatter(inward_grad, ('dp', 'seq'), scatter_dimension=0, tiled=T...  177 us
    unnamed x16, waiting for transfers between devices  171 us
    reduce_scatter x1, waiting for transfers between devices, body(): lax.psum_scatter(outward_grad, ('dp', 'seq'), scatter_dimension=0, tiled=...  138 us
    all_gather x1, waiting for transfers between devices, body(): lax.all_gather(halved(shrink), ('dp', 'seq'), axis=0, tiled=True)  74.2 us
    all_gather x1, waiting for transfers between devices, body(): lax.all_gather(halved(expand), ('dp', 'seq'), axis=0, tiled=True)  70 us
  transfers between devices with their start and end apart: 19, of which 13 were waited for; matrix products, arithmetic and copies ran while one was open for 6% of the time, Pallas kernels for 0%

profile of v1, /device:TPU:9, one launch (start us, length us, event | category | flops | bytes accessed | tf_op | source)
XLA Modules:
  0.0 1614.5 jit_solution(2311156718169087570)
XLA Ops:
  12.1 35.6 %all-gather = bf16[32,32,5]{1,2,0:T(8,128)(2,1)S(1)} all-gather(bf16[1,32,5]{1,2,0:T(8,128)(2,1)S(1)} %convert_bitcast_fusion), channel_id=1, replica_groups=mesh['dp'=8,'seq'=4] {'dp','seq'}, dimensions={0}, use_global_device_ids=true | all-gather | bytes 10560 | tf_op jit(solution)/shard_map/all_gather | solution.py:122
  49.2 13.5 collective-permute-done.1
  63.0 26.4 %all-gather.10.cloned.1.call-done = bf16[1024,3072]{1,0:T(8,128)(2,1)} async-done(((bf16[32,3072]{1,0:T(8,128)(2,1)}), bf16[1024,3072]{1,0:T(8,128)(2,1)}) %all-gather.10.cloned.1.call-update) | async-done | bytes 6291472 | tf_op jit(solution)/shard_map/all_gather | solution.py:121
  104.7 40.5 %collective-permute-done.3 = bf16[256,4096]{1,0:T(8,128)(2,1)} collective-permute-done((bf16[256,4096]{1,0:T(8,128)(2,1)S(1)}, bf16[256,4096]{1,0:T(8,128)(2,1)}, u32[]{:S(2)}, u32[]{:S(2)}) %collective-permute-start.3) | collective-permute-done | bytes 2097184 | tf_op jit(solution)/shard_map/ppermute | solution.py:29
  151.8 208.6 %all-gather.1 = bf16[32,32,3]{1,2,0:T(4,128)(2,1)S(1)} all-gather(bf16[1,32,3]{1,2,0:T(4,128)(2,1)S(1)} %convert_bitcast_fusion.1), channel_id=1, replica_groups=mesh['dp'=8,'seq'=4] {'dp','seq'}, dimensions={0}, use_global_device_ids=true | all-gather | bytes 6336 | tf_op jit(solution)/shard_map/all_gather | solution.py:167
  360.5 32.0 %all-gather.2 = bf16[32,1,128]{2,1,0:T(2,128)(2,1)S(1)} all-gather(bf16[1,1,128]{2,1,0:T(2,128)(2,1)S(1)} %convert_bitcast_fusion.2), channel_id=1, replica_groups=mesh['dp'=8,'seq'=4] {'dp','seq'}, dimensions={0}, use_global_device_ids=true | all-gather | bytes 8448 | tf_op jit(solution)/shard_map/all_gather | solution.py:172
  411.8 7.6 fusion.7
  420.8 8.2 fusion.58
  429.1 187.7 %reduce-scatter.23.cloned.1.call-done = f32[128,1024]{1,0:T(8,128)} async-done(((f32[4096,1024]{1,0:T(8,128)}), f32[128,1024]{1,0:T(8,128)}) %reduce-scatter.23.cloned.1.call-update) | async-done | bytes 524304 | tf_op jit(solution)/shard_map/reduce_scatter | solution.py:208
  622.5 74.2 %all-gather.18.cloned.1.call-done = bf16[4096,1024]{1,0:T(8,128)(2,1)} async-done(((bf16[128,1024]{1,0:T(8,128)(2,1)}), bf16[4096,1024]{1,0:T(8,128)(2,1)}) %all-gather.18.cloned.1.call-update) | async-done | bytes 8388624 | tf_op jit(solution)/shard_map/all_gather | solution.py:171
  696.7 9.1 fusion.69
  705.8 70.0 %all-gather.20.cloned.1.call-done = bf16[1024,4096]{1,0:T(8,128)(2,1)} async-done(((bf16[32,4096]{1,0:T(8,128)(2,1)}), bf16[1024,4096]{1,0:T(8,128)(2,1)}) %all-gather.20.cloned.1.call-update) | async-done | bytes 8388624 | tf_op jit(solution)/shard_map/all_gather | solution.py:199
  775.8 7.3 multiply_reduce_fusion.1
  807.7 10.9 reduce-scatter.15.cloned.1.call-done
  818.6 27.4 %reduce-scatter.13.cloned.1.call-done = bf16[2,64,1024]{2,1,0:T(8,128)(2,1)} async-done(((bf16[2,256,1024]{2,1,0:T(8,128)(2,1)}), bf16[2,64,1024]{2,1,0:T(8,128)(2,1)}) %reduce-scatter.13.cloned.1.call-update) | async-done | bytes 262160 | tf_op jit(solution)/shard_map/reduce_scatter | solution.py:248
  856.8 6.4 fusion.27
  864.5 8.3 fusion.22
  875.0 38.7 %all-reduce = f32[4096]{0:T(1024)S(1)} all-reduce(f32[4096]{0:T(1024)S(1)} %copy-done.45), channel_id=10, replica_groups=mesh['dp'=8,'seq'=4] {'dp','seq'}, use_global_device_ids=true, to_apply=%region_29.30.clone | all-reduce | flops 4096 | bytes 32768
  915.0 6.4 fusion.16
  921.4 39.6 %reduce-scatter.27.cloned.1.call-done = f32[32,3]{1,0:T(8,128)} async-done(((f32[1024,3]{1,0:T(8,128)}), f32[32,3]{1,0:T(8,128)}) %reduce-scatter.27.cloned.1.call-update) | async-done | bytes 400
  964.5 130.9 %reduce-scatter.25.cloned.1.call-done = f32[32,5]{1,0:T(8,128)} async-done(((f32[1024,5]{1,0:T(8,128)}), f32[32,5]{1,0:T(8,128)}) %reduce-scatter.25.cloned.1.call-update) | async-done | bytes 656
  1097.5 138.4 %reduce-scatter.19.cloned.1.call-done = f32[32,1024]{1,0:T(8,128)} async-done(((f32[1024,1024]{1,0:T(8,128)}), f32[32,1024]{1,0:T(8,128)}) %reduce-scatter.19.cloned.1.call-update) | async-done | bytes 131088 | tf_op jit(solution)/shard_map/reduce_scatter | solution.py:275
  1238.3 176.7 %reduce-scatter.17.cloned.1.call-done = f32[32,3072]{1,0:T(8,128)} async-done(((f32[1024,3072]{1,0:T(8,128)}), f32[32,3072]{1,0:T(8,128)}) %reduce-scatter.17.cloned.1.call-update) | async-done | bytes 393232 | tf_op jit(solution)/shard_map/reduce_scatter | solution.py:274
  1418.0 186.7 %reduce-scatter.21.cloned.1.call-done = f32[32,4096]{1,0:T(8,128)} async-done(((f32[1024,4096]{1,0:T(8,128)}), f32[32,4096]{1,0:T(8,128)}) %reduce-scatter.21.cloned.1.call-update) | async-done | bytes 524304 | tf_op jit(solution)/shard_map/reduce_scatter | solution.py:207
  (284 shorter events, 108.5 us)
Async XLA Ops:
  7.2 82.2 %all-gather.10.cloned.1.call-start = ((), (), s32[]{:S(2)}) async-start(), calls=%async_computation.8 | async-start | bytes 6488064 | tf_op jit(solution)/shard_map/all_gather | solution.py:121
  9.0 389.1 %all-gather.12.cloned.1.call-start = ((), (), s32[]{:S(2)}) async-start(), calls=%async_computation.9 | async-start | bytes 1310720 | tf_op jit(solution)/shard_map/all_gather | solution.py:137
  10.2 37.9 %collective-permute-start = (bf16[32,4096]{1,0:T(8,128)(2,1)S(1)}, bf16[32,4096]{1,0:T(8,128)(2,1)S(1)}, u32[]{:S(2)}, u32[]{:S(2)}) collective-permute-start(bf16[32,4096]{1,0:T(8,128)(2,1)S(1)} %convert_element_type.131), channel_id=1, source_target_pairs={{0,1},{1,0},{2,3},{3,2},{4,5},{5,4},{6,7},{7,6},{8,9},{9,8},{10,11... | collective-permute-start | bytes 786440 | tf_op jit(solution)/shard_map/ppermute | solution.py:29
  48.1 14.5 collective-permute-start.1
  62.9 32.4 %collective-permute-start.2 = (bf16[128,4096]{1,0:T(8,128)(2,1)S(1)}, bf16[128,4096]{1,0:T(8,128)(2,1)}, u32[]{:S(2)}, u32[]{:S(2)}) collective-permute-start(bf16[128,4096]{1,0:T(8,128)(2,1)S(1)} %maximum_select_fusion.6), channel_id=1, source_target_pairs={{0,4},{1,5},{2,6},{3,7},{4,0},{5,1},{6,2},{7,3},{8,12},{9,13},{10,... | collective-permute-start | bytes 3145736 | tf_op jit(solution)/shard_map/ppermute | solution.py:29
  95.2 305.4 %all-gather.14.cloned.1.call-start = ((), (), s32[]{:S(2)}) async-start(), calls=%async_computation.10 | async-start | bytes 1310720 | tf_op jit(solution)/shard_map/all_gather | solution.py:136
  98.3 46.9 %collective-permute-start.3 = (bf16[256,4096]{1,0:T(8,128)(2,1)S(1)}, bf16[256,4096]{1,0:T(8,128)(2,1)}, u32[]{:S(2)}, u32[]{:S(2)}) collective-permute-start(bf16[256,4096]{1,0:T(8,128)(2,1)S(1)} %maximum_select_fusion.5), channel_id=1, source_target_pairs={{0,8},{1,9},{2,10},{3,11},{4,12},{5,13},{6,14},{7,15},{8,0},{9,1},... | collective-permute-start | bytes 6291464 | tf_op jit(solution)/shard_map/ppermute | solution.py:29
  103.9 305.5 %all-gather.16.cloned.1.call-start = ((), (), s32[]{:S(2)}) async-start(), calls=%async_computation.11 | async-start | bytes 2162688 | tf_op jit(solution)/shard_map/all_gather | solution.py:158
  104.6 512.2 %reduce-scatter.23.cloned.1.call-start = ((), (), s32[]{:S(2)}) async-start(), calls=%async_computation.19 | async-start | bytes 17301504 | tf_op jit(solution)/shard_map/reduce_scatter | solution.py:208
  150.1 261.7 %collective-permute-start.4 = (bf16[512,4096]{1,0:T(8,128)(2,1)}, bf16[512,4096]{1,0:T(8,128)(2,1)}, u32[]{:S(2)}, u32[]{:S(2)}) collective-permute-start(bf16[512,4096]{1,0:T(8,128)(2,1)} %maximum_select_fusion.4), channel_id=1, source_target_pairs={{0,16},{1,17},{2,18},{3,19},{4,20},{5,21},{6,22},{7,23},{8,24},{9,... | collective-permute-start | bytes 12582920 | tf_op jit(solution)/shard_map/ppermute | solution.py:29
  429.0 267.7 %all-gather.18.cloned.1.call-start = ((), (), s32[]{:S(2)}) async-start(), calls=%async_computation.12 | async-start | bytes 8650752 | tf_op jit(solution)/shard_map/all_gather | solution.py:171
  620.0 155.8 %all-gather.20.cloned.1.call-start = ((), (), s32[]{:S(2)}) async-start(), calls=%async_computation.13 | async-start | bytes 8650752 | tf_op jit(solution)/shard_map/all_gather | solution.py:199
  620.8 197.8 %reduce-scatter.15.cloned.1.call-start = ((), (), s32[]{:S(2)}) async-start(), calls=%async_computation.15 | async-start | bytes 1310720 | tf_op jit(solution)/shard_map/reduce_scatter | solution.py:251
  795.6 50.3 %reduce-scatter.13.cloned.1.call-start = ((), (), s32[]{:S(2)}) async-start(), calls=%async_computation.14 | async-start | bytes 1310720 | tf_op jit(solution)/shard_map/reduce_scatter | solution.py:248
  804.3 156.7 %reduce-scatter.27.cloned.1.call-start = ((), (), s32[]{:S(2)}) async-start(), calls=%async_computation.21 | async-start | bytes 540672
  807.4 288.1 %reduce-scatter.25.cloned.1.call-start = ((), (), s32[]{:S(2)}) async-start(), calls=%async_computation.20 | async-start | bytes 540672
  853.1 382.8 %reduce-scatter.19.cloned.1.call-start = ((), (), s32[]{:S(2)}) async-start(), calls=%async_computation.17 | async-start | bytes 4325376 | tf_op jit(solution)/shard_map/reduce_scatter | solution.py:275
  855.9 559.1 %reduce-scatter.17.cloned.1.call-start = ((), (), s32[]{:S(2)}) async-start(), calls=%async_computation.16 | async-start | bytes 12976128 | tf_op jit(solution)/shard_map/reduce_scatter | solution.py:274
  863.3 741.4 %reduce-scatter.21.cloned.1.call-start = ((), (), s32[]{:S(2)}) async-start(), calls=%async_computation.18 | async-start | bytes 17301504 | tf_op jit(solution)/shard_map/reduce_scatter | solution.py:207
  963.3 451.7 %copy-start.22 = (f32[32,3072]{1,0:T(8,128)S(1)}, f32[32,3072]{1,0:T(8,128)}, u32[]{:S(2)}) copy-start(f32[32,3072]{1,0:T(8,128)} %param.20) | copy-start | bytes 1179652
  963.3 451.7 %copy-start.26 = (f32[2,32,3072]{2,1,0:T(8,128)S(1)}, f32[2,32,3072]{2,1,0:T(8,128)}, u32[]{:S(2)}) copy-start(f32[2,32,3072]{2,1,0:T(8,128)} %param.27) | copy-start | bytes 2359300
  1096.2 320.8 %copy-start.42 = (f32[32,5]{0,1:T(8,128)}, f32[32,5]{0,1:T(8,128)S(1)}, u32[]{:S(2)}) copy-start(f32[32,5]{0,1:T(8,128)S(1)} %copy.118) | copy-start | bytes 1924
  1238.3 366.4 %copy-start.19 = (f32[32,4096]{1,0:T(8,128)S(1)}, f32[32,4096]{1,0:T(8,128)}, u32[]{:S(2)}) copy-start(f32[32,4096]{1,0:T(8,128)} %param.23) | copy-start | bytes 1572868
  1238.3 366.4 %copy-start.24 = (f32[2,32,4096]{2,1,0:T(8,128)S(1)}, f32[2,32,4096]{2,1,0:T(8,128)}, u32[]{:S(2)}) copy-start(f32[2,32,4096]{2,1,0:T(8,128)} %param.30) | copy-start | bytes 3145732
  (69 other events, 1975.3 us)
Sparse Core Ops, SparseCore 0:
  11.5 77.8 all-gather.9
  95.3 16.8 all-gather.11
  114.4 16.6 all-gather.13
  134.4 222.5 all-gather.15
  429.1 187.5 reduce-scatter.22
  620.2 76.4 all-gather.17
  700.1 75.6 all-gather.19
  795.8 22.7 reduce-scatter.14
  821.1 24.7 reduce-scatter.12
  848.6 112.3 reduce-scatter.26
  963.8 131.5 reduce-scatter.24
  1098.1 137.7 reduce-scatter.18
  1242.5 172.4 reduce-scatter.16
  1417.7 186.9 reduce-scatter.20
